TPU v7x, 32 devices: a whole 2x2x4 slice. The times are simulated.
32 devices in a mesh: paths: 4 (over y, core), factors: 8 (over z, x).
Axes of the slice: x: 2, y: 2, z: 4, core: 2. Of those that a mesh axis runs over, the one named last changes fastest.
Arguments:
- x_start: float32 [512, 2048], P('factors', 'paths'), may hold values from -3 to 3
- shocks: float32 [4, 512, 2048], P(None, 'factors', 'paths'), may hold values from -6 to 6
- cholesky: float32 [512, 512], P(None, 'factors'), as said below
- reversion: float32 [512], P('factors'), may hold values from 0.05 to 2
- sabr_alpha: float32 [64], replicated, may hold values from 0.2 to 0.6
- sabr_rho: float32 [64], replicated, may hold values from -0.7 to 0.7
- sabr_nu: float32 [64], replicated, may hold values from 0.3 to 1.5
- factor_slice: int32 [512], P('factors'), may hold values from 0 to 63
- notional: float32 [32768], P('factors'), may hold values from -1 to 1
- strike: float32 [32768], P('factors'), may hold values from -3 to 3
- trade_set: int32 [32768], P('factors'), may hold values from 0 to 255
- trade_factor: int32 [32768], P('factors'), may hold values from 0 to 511, as said below
- loss_given: float32 [256], replicated, may hold values from 0.2 to 0.8
Outputs:
- path_adjoint: float32 [512, 2048], P('factors', 'paths')
- sabr_grad: float32 [3, 64], replicated
Inputs may be any that keep to these rules, and one draw needn't show every extreme that they name: `cholesky`: lower triangular with a positive diagonal and rows of unit length. `trade_factor`: trade t's factor lies in [(t // 4096) * 64, (t // 4096 + 1) * 64).
All inputs are finite; a program needn't handle non-finite values.
Results may differ from a plain program's by a relative error of at most 0.004.
Values may be sent and summed in bfloat16 or wider, within the bound.
A program may use at most 192 MiB of HBM per device.

v0:
```python
import math
import jax
import jax.numpy as jnp
from jax import lax
from jax.sharding import PartitionSpec as P

TIME_STEP = 0.25
ROOT_STEP = 0.5
DISCOUNT_RATE = 0.03
PRECISE = lax.Precision.HIGHEST
CONTRACT_FIRST = (((0,), (0,)), ((), ()))


def shortened(value):
    return jax.tree.map(lambda a: a.astype(jnp.bfloat16) if a.dtype == jnp.float32 else a, value)


def smile_terms(squashed, alpha_rows, rho_rows, nu_rows):
    curve = (2.0 - 3.0 * rho_rows * rho_rows) * nu_rows * nu_rows / 24.0
    base = 1.0 + 0.5 * rho_rows * nu_rows * squashed + curve * squashed * squashed
    rho_slope = alpha_rows * (
        0.5 * nu_rows * squashed - 0.25 * rho_rows * nu_rows * nu_rows * squashed * squashed
    )
    nu_slope = alpha_rows * (
        0.5 * rho_rows * squashed
        + (2.0 - 3.0 * rho_rows * rho_rows) * nu_rows * squashed * squashed / 12.0
    )
    level_slope = alpha_rows * (0.5 * rho_rows * nu_rows + 2.0 * curve * squashed)
    return (alpha_rows * base, base, rho_slope, nu_slope, level_slope)


def split_factors(
    x_start,
    shocks,
    cholesky,
    reversion,
    sabr_alpha,
    sabr_rho,
    sabr_nu,
    factor_slice,
    notional,
    strike,
    trade_set,
    trade_factor,
    loss_given,
):
    factor_rows, path_cols = x_start.shape
    step_count = shocks.shape[0]
    total_sets = loss_given.shape[0]
    factor_place = lax.axis_index("factors")
    slice_count = sabr_alpha.shape[0]
    slice_table = (
        factor_slice[:, None] == jnp.arange(slice_count, dtype=jnp.int32)[None, :]
    ).astype(jnp.float32)
    alpha_rows = jnp.dot(slice_table, sabr_alpha, precision=PRECISE)[:, None]
    rho_rows = jnp.dot(slice_table, sabr_rho, precision=PRECISE)[:, None]
    nu_rows = jnp.dot(slice_table, sabr_nu, precision=PRECISE)[:, None]
    local_factor = trade_factor - factor_place * factor_rows
    factor_table = (
        jnp.arange(factor_rows, dtype=jnp.int32)[:, None] == local_factor[None, :]
    ).astype(jnp.float32)
    set_table = (jnp.arange(total_sets, dtype=jnp.int32)[:, None] == trade_set[None, :]).astype(
        jnp.bfloat16
    )
    damping = (1.0 - reversion * TIME_STEP)[:, None]
    state = x_start
    states = [state]
    weights = []
    for step_index in range(step_count):
        squashed = jnp.tanh(state)
        local_vol = smile_terms(squashed, alpha_rows, rho_rows, nu_rows)[0]
        correlate_source = local_vol * shocks[step_index]
        mixed = lax.psum_scatter(
            jnp.dot(cholesky, correlate_source, precision=PRECISE),
            "factors",
            scatter_dimension=0,
            tiled=True,
        )
        state = damping * state + ROOT_STEP * mixed
        states.append(state)
        moneyness = jnp.take(state, local_factor, axis=0) - strike[:, None]
        values = (notional[:, None] * jnp.tanh(moneyness)).astype(jnp.bfloat16)
        discount = math.exp(-DISCOUNT_RATE * TIME_STEP * (step_index + 1))
        partial_sum = jnp.dot(set_table, values, preferred_element_type=jnp.float32)
        exposure = lax.psum(partial_sum.astype(jnp.bfloat16), "factors").astype(jnp.float32)
        weights.append(
            (discount * loss_given[:, None] * jax.nn.sigmoid(exposure)).astype(jnp.bfloat16)
        )
    adjoint = jnp.zeros_like(x_start)
    factor_sums = jnp.zeros((3, factor_rows), jnp.float32)
    for step_index in reversed(range(step_count)):
        moneyness = jnp.take(states[step_index + 1], local_factor, axis=0) - strike[:, None]
        squash_trade = jnp.tanh(moneyness)
        trade_term = (
            notional[:, None]
            * (1.0 - squash_trade * squash_trade)
            * lax.dot_general(
                set_table, weights[step_index], CONTRACT_FIRST, preferred_element_type=jnp.float32
            )
        )
        adjoint = adjoint + jnp.dot(factor_table, trade_term, precision=PRECISE)
        shock_adjoint = jnp.zeros((factor_rows, path_cols), jnp.float32) + lax.dot_general(
            cholesky,
            lax.all_gather(shortened(ROOT_STEP * adjoint), "factors", axis=0, tiled=True),
            CONTRACT_FIRST,
            precision=PRECISE,
        )
        squashed = jnp.tanh(states[step_index])
        local_vol, base, rho_slope, nu_slope, level_slope = smile_terms(
            squashed, alpha_rows, rho_rows, nu_rows
        )
        vol_adjoint = shock_adjoint * shocks[step_index]
        factor_sums = factor_sums + jnp.stack(
            [
                jnp.sum(vol_adjoint * base, axis=1),
                jnp.sum(vol_adjoint * rho_slope, axis=1),
                jnp.sum(vol_adjoint * nu_slope, axis=1),
            ]
        )
        adjoint = damping * adjoint + vol_adjoint * level_slope * (1.0 - squashed * squashed)
    slice_sums = jnp.dot(factor_sums, slice_table, precision=PRECISE)
    return (adjoint, slice_sums)


def per_device(
    x_start,
    shocks,
    cholesky,
    reversion,
    sabr_alpha,
    sabr_rho,
    sabr_nu,
    factor_slice,
    notional,
    strike,
    trade_set,
    trade_factor,
    loss_given,
):
    adjoint, slice_sums = split_factors(
        x_start,
        shocks,
        cholesky,
        reversion,
        sabr_alpha,
        sabr_rho,
        sabr_nu,
        factor_slice,
        notional,
        strike,
        trade_set,
        trade_factor,
        loss_given,
    )
    total_grad = lax.psum(slice_sums, ("paths", "factors"))
    sabr_grad = total_grad / (x_start.shape[1] * lax.axis_size("paths"))
    return (adjoint, sabr_grad)


def solution(mesh):
    return jax.shard_map(
        per_device,
        mesh=mesh,
        in_specs=(
            P("factors", "paths"),
            P(None, "factors", "paths"),
            P(None, "factors"),
            P("factors"),
            P(),
            P(),
            P(),
            P("factors"),
            P("factors"),
            P("factors"),
            P("factors"),
            P("factors"),
            P(),
        ),
        out_specs=(P("factors", "paths"), P()),
        check_vma=False,
    )
```

profile of v0, /device:TPU:0, one launch (start us, length us, event | category | flops | bytes accessed | tf_op | source)
XLA Modules:
  0.0 588.1 jit_solution(14679514657513539477)
XLA Ops:
  7.2 0.0 copy-start
  7.2 0.0 copy-start.2
  7.2 0.0 reduce-scatter.13.cloned.1.call-start
  7.2 0.9 convolution_bitcast_fusion.9
  8.2 0.9 convolution_bitcast_fusion.10
  9.1 0.9 broadcast_multiply_fusion.5
  10.0 2.1 convolution_bitcast_fusion.3
  12.1 1.3 copy.39
  13.4 0.0 reduce-scatter.13.cloned.1.call-update
  13.5 0.0 reduce-scatter.15.cloned.1.call-start
  13.5 0.7 multiply_subtract_fusion
  14.2 66.8 %reduce-scatter.13.cloned.1.call-done = f32[64,512]{1,0:T(8,128)} async-done(((f32[512,512]{1,0:T(8,128)}), f32[64,512]{1,0:T(8,128)}) %reduce-scatter.13.cloned.1.call-update) | async-done | bytes 131088 | tf_op jit(solution)/shard_map/reduce_scatter | solution.py:73
  80.9 1.0 multiply_add_fusion.4
  82.0 2.0 convolution_bitcast_fusion.2
  84.0 1.3 copy.41
  85.3 0.0 reduce-scatter.15.cloned.1.call-update
  85.4 0.0 reduce-scatter.17.cloned.1.call-start
  85.4 63.6 %reduce-scatter.15.cloned.1.call-done = f32[64,512]{1,0:T(8,128)} async-done(((f32[512,512]{1,0:T(8,128)}), f32[64,512]{1,0:T(8,128)}) %reduce-scatter.15.cloned.1.call-update) | async-done | bytes 131088 | tf_op jit(solution)/shard_map/reduce_scatter | solution.py:73
  149.0 1.0 multiply_add_fusion.3
  150.0 1.1 convolution_bitcast_fusion.1
  151.1 1.4 copy.43
  152.5 0.0 reduce-scatter.17.cloned.1.call-update
  152.6 0.0 reduce-scatter.19.cloned.1.call-start
  152.7 0.0 copy-start.3
  152.7 0.0 copy-start.10
  152.7 16.8 %gather_fusion.3 = f32[4096,512]{1,0:T(8,128)} fusion(f32[64,512]{1,0:T(8,128)S(1)} %multiply_add_fusion.4, s32[4096]{0:T(1024)S(1)} %fusion.166), kind=kCustom, calls=%fused_computation.3.clone | custom fusion | bytes 16793600 | tf_op jit(solution)/shard_map/jit(_take)/gather | solution.py:92
  169.5 46.4 %reduce-scatter.17.cloned.1.call-done = f32[64,512]{1,0:T(8,128)} async-done(((f32[512,512]{1,0:T(8,128)}), f32[64,512]{1,0:T(8,128)}) %reduce-scatter.17.cloned.1.call-update) | async-done | bytes 131088 | tf_op jit(solution)/shard_map/reduce_scatter | solution.py:73
  215.9 1.0 multiply_add_fusion.2
  216.8 1.1 convolution_bitcast_fusion
  218.0 1.4 copy.45
  219.4 0.0 reduce-scatter.19.cloned.1.call-update
  219.4 0.3 all-reduce.3.cloned.1.call-start
  219.8 6.3 %fusion.67 = bf16[256,512]{1,0:T(8,128)(2,1)} fusion(f32[4096,512]{1,0:T(8,128)} %gather_fusion.3, f32[4096]{0:T(1024)S(1)} %copy-done.10, f32[4096]{0:T(1024)S(1)} %copy-done.11, pred[4096]{0:T(1024)(128)(4,1)S(1)} %get-tuple-element.32, s32[4096]{0:T(1024)S(1)} %copy-done.3), kind=kOutput, calls=%fused_computation.80 | convolution fusion | flops 1083310080 | bytes 8704000 | tf_op jit(solution)/shard_map/dot_general | solution.py:84
  226.1 16.8 %gather_fusion.2 = f32[4096,512]{1,0:T(8,128)} fusion(f32[64,512]{1,0:T(8,128)S(1)} %multiply_add_fusion.3, s32[4096]{0:T(1024)S(1)} %fusion.166), kind=kCustom, calls=%fused_computation.2.clone | custom fusion | bytes 16793600 | tf_op jit(solution)/shard_map/jit(_take)/gather | solution.py:92
  242.9 6.3 %fusion.66 = bf16[256,512]{1,0:T(8,128)(2,1)} fusion(f32[4096,512]{1,0:T(8,128)} %gather_fusion.2, f32[4096]{0:T(1024)S(1)} %copy-done.10, f32[4096]{0:T(1024)S(1)} %copy-done.11, pred[4096]{0:T(1024)(128)(4,1)S(1)} %get-tuple-element.32, s32[4096]{0:T(1024)S(1)} %copy-done.3), kind=kOutput, calls=%fused_computation.79 | convolution fusion | flops 1083310080 | bytes 8704000 | tf_op jit(solution)/shard_map/dot_general | solution.py:84
  249.2 16.8 %gather_fusion.1 = f32[4096,512]{1,0:T(8,128)} fusion(f32[64,512]{1,0:T(8,128)S(1)} %multiply_add_fusion.2, s32[4096]{0:T(1024)S(1)} %fusion.166), kind=kCustom, calls=%fused_computation.1.clone | custom fusion | bytes 16793600 | tf_op jit(solution)/shard_map/jit(_take)/gather | solution.py:92
  266.0 6.4 %fusion.65 = bf16[256,512]{1,0:T(8,128)(2,1)} fusion(f32[4096,512]{1,0:T(8,128)} %gather_fusion.1, f32[4096]{0:T(1024)S(1)} %copy-done.10, f32[4096]{0:T(1024)S(1)} %copy-done.11, pred[4096]{0:T(1024)(128)(4,1)S(1)} %get-tuple-element.32, s32[4096]{0:T(1024)S(1)} %copy-done.3), kind=kOutput, calls=%fused_computation.78 | convolution fusion | flops 1083310080 | bytes 8704000 | tf_op jit(solution)/shard_map/dot_general | solution.py:84
  272.3 10.4 %reduce-scatter.19.cloned.1.call-done = f32[64,512]{1,0:T(8,128)} async-done(((f32[512,512]{1,0:T(8,128)}), f32[64,512]{1,0:T(8,128)}) %reduce-scatter.19.cloned.1.call-update) | async-done | bytes 131088 | tf_op jit(solution)/shard_map/reduce_scatter | solution.py:73
  282.7 1.0 multiply_add_fusion.1
  283.7 16.8 %gather_fusion = f32[4096,512]{1,0:T(8,128)} fusion(f32[64,512]{1,0:T(8,128)S(1)} %multiply_add_fusion.1, s32[4096]{0:T(1024)S(1)} %fusion.166), kind=kCustom, calls=%fused_computation.clone | custom fusion | bytes 16793600 | tf_op jit(solution)/shard_map/jit(_take)/gather | solution.py:92
  300.5 6.3 %fusion.64 = bf16[256,512]{1,0:T(8,128)(2,1)} fusion(f32[4096,512]{1,0:T(8,128)} %gather_fusion, f32[4096]{0:T(1024)S(1)} %copy-done.10, f32[4096]{0:T(1024)S(1)} %copy-done.11, pred[4096]{0:T(1024)(128)(4,1)S(1)} %get-tuple-element.32, s32[4096]{0:T(1024)S(1)} %copy-done.3), kind=kOutput, calls=%fused_computation.77 | convolution fusion | flops 1083310080 | bytes 8704000 | tf_op jit(solution)/shard_map/dot_general | solution.py:84
  306.9 0.0 all-reduce.3.cloned.1.call-update
  306.9 77.6 %all-reduce.3.cloned.1.call-done = (bf16[256,512]{1,0:T(8,128)(2,1)}, bf16[256,512]{1,0:T(8,128)(2,1)}, bf16[256,512]{1,0:T(8,128)(2,1)}, bf16[256,512]{1,0:T(8,128)(2,1)}) async-done(((bf16[256,512]{1,0:T(8,128)(2,1)}, bf16[256,512]{1,0:T(8,128)(2,1)}, bf16[256,512]{1,0:T(8,128)(2,1)}, bf16[256,512]{1,0:T(8,128)(2,1)}), (bf16[256,512]{1,0:T(8,128)(2,1)}, bf16[256,512]{1,0:T(8,128)(2,1)}, ...) | async-done | bytes 1048592 | tf_op jit(solution)/shard_map/psum | solution.py:85
  384.5 2.5 fusion.38
  387.0 1.0 copy-done.1
  387.9 5.4 multiply_convert_fusion.27
  393.3 31.8 %all_gather.12 = bf16[512,512]{1,0:T(8,128)(2,1)S(1)} all-gather(bf16[64,512]{1,0:T(8,128)(2,1)S(1)} %get-tuple-element.45), channel_id=1, replica_groups=mesh['paths'=4,'factors'=8] {'factors'}, dimensions={0}, use_global_device_ids=true | all-gather | bytes 589824 | tf_op jit(solution)/shard_map/all_gather | solution.py:104
  425.1 0.4 fusion.71
  425.5 1.4 fusion.36
  427.0 5.4 multiply_convert_fusion.26
  432.3 31.6 %all_gather.13 = bf16[512,512]{1,0:T(8,128)(2,1)S(1)} all-gather(bf16[64,512]{1,0:T(8,128)(2,1)S(1)} %get-tuple-element.47), channel_id=1, replica_groups=mesh['paths'=4,'factors'=8] {'factors'}, dimensions={0}, use_global_device_ids=true | all-gather | bytes 589824 | tf_op jit(solution)/shard_map/all_gather | solution.py:104
  463.9 0.4 fusion.70
  464.3 1.4 fusion.34
  465.8 5.4 multiply_convert_fusion.25
  471.2 31.5 %all_gather.14 = bf16[512,512]{1,0:T(8,128)(2,1)S(1)} all-gather(bf16[64,512]{1,0:T(8,128)(2,1)S(1)} %get-tuple-element.49), channel_id=1, replica_groups=mesh['paths'=4,'factors'=8] {'factors'}, dimensions={0}, use_global_device_ids=true | all-gather | bytes 589824 | tf_op jit(solution)/shard_map/all_gather | solution.py:104
  502.7 0.4 fusion.69
  503.1 1.4 fusion.32
  504.5 0.0 copy-start.4
  504.5 5.4 multiply_convert_fusion.24
  509.9 31.2 %all_gather.15 = bf16[512,512]{1,0:T(8,128)(2,1)S(1)} all-gather(bf16[64,512]{1,0:T(8,128)(2,1)S(1)} %get-tuple-element.51), channel_id=1, replica_groups=mesh['paths'=4,'factors'=8] {'factors'}, dimensions={0}, use_global_device_ids=true | all-gather | bytes 589824 | tf_op jit(solution)/shard_map/all_gather | solution.py:104
  541.1 1.6 fusion.100
  542.7 0.2 fusion.161
  542.9 37.8 %psum.39 = f32[3,64]{1,0:T(4,128)S(1)} all-reduce(f32[3,64]{1,0:T(4,128)S(1)} %fusion.161), channel_id=1, replica_groups=mesh['paths'=4,'factors'=8] {'paths','factors'}, use_global_device_ids=true, to_apply=%region_20.22 | all-reduce | flops 192 | bytes 1536 | tf_op jit(solution)/shard_map/psum | solution.py:155
  580.8 0.6 broadcast_multiply_fusion
  (39 shorter events, 0.1 us)
Async XLA Ops:
  7.2 2.8 copy-start
  7.2 142.8 %copy-start.2 = (f32[4,64,512]{2,1,0:T(8,128)S(1)}, f32[4,64,512]{2,1,0:T(8,128)}, u32[]{:S(2)}) copy-start(f32[4,64,512]{2,1,0:T(8,128)} %param.16) | copy-start | bytes 1572868
  7.2 145.4 %copy-start.8 = (s32[4096]{0:T(1024)S(1)}, s32[4096]{0:T(1024)}, u32[]{:S(2)}) copy-start(s32[4096]{0:T(1024)} %param.26) | copy-start | bytes 49156
  7.2 73.7 %reduce-scatter.13.cloned.1.call-start = ((), (), s32[]{:S(2)}) async-start(), calls=%async_computation.4 | async-start | bytes 1179648 | tf_op jit(solution)/shard_map/reduce_scatter | solution.py:73
  13.5 135.6 %reduce-scatter.15.cloned.1.call-start = ((), (), s32[]{:S(2)}) async-start(), calls=%async_computation.5 | async-start | bytes 1179648 | tf_op jit(solution)/shard_map/reduce_scatter | solution.py:73
  85.4 130.5 %reduce-scatter.17.cloned.1.call-start = ((), (), s32[]{:S(2)}) async-start(), calls=%async_computation.6 | async-start | bytes 1179648 | tf_op jit(solution)/shard_map/reduce_scatter | solution.py:73
  152.6 130.2 %reduce-scatter.19.cloned.1.call-start = ((), (), s32[]{:S(2)}) async-start(), calls=%async_computation.7 | async-start | bytes 1179648 | tf_op jit(solution)/shard_map/reduce_scatter | solution.py:73
  152.7 67.1 %copy-start.3 = (s32[4096]{0:T(1024)S(1)}, s32[4096]{0:T(1024)}, u32[]{:S(2)}) copy-start(s32[4096]{0:T(1024)} %param.25) | copy-start | bytes 49156
  152.7 67.1 %copy-start.10 = (f32[4096]{0:T(1024)S(1)}, f32[4096]{0:T(1024)}, u32[]{:S(2)}) copy-start(f32[4096]{0:T(1024)} %param.24) | copy-start | bytes 49156
  152.7 67.1 %copy-start.11 = (f32[4096]{0:T(1024)S(1)}, f32[4096]{0:T(1024)}, u32[]{:S(2)}) copy-start(f32[4096]{0:T(1024)} %param.23) | copy-start | bytes 49156
  219.4 165.1 %all-reduce.3.cloned.1.call-start = ((), (), s32[]{:S(2)}) async-start(), calls=%async_computation.8 | async-start | bytes 2097152 | tf_op jit(solution)/shard_map/psum | solution.py:85
  300.5 6.4 %copy-start.9 = (f32[256]{0:T(256)S(1)}, f32[256]{0:T(256)}, u32[]{:S(2)}) copy-start(f32[256]{0:T(256)} %param.27) | copy-start | bytes 3076
  384.5 3.5 copy-start.1
  384.5 42.4 %slice-start.4 = ((s8[8388608]{0:T(1024)(128)(4,1)}), s8[4194304]{0:T(1024)(128)(4,1)S(1)}, s32[]{:S(2)}) async-start(s8[8388608]{0:T(1024)(128)(4,1)} %bitcast.89), calls=%async_computation.13 | async-start | bytes 8388608
  387.9 37.6 %copy-start.7 = (bf16[256,512]{1,0:T(8,128)(2,1)S(1)}, bf16[256,512]{1,0:T(8,128)(2,1)}, u32[]{:S(2)}) copy-start(bf16[256,512]{1,0:T(8,128)(2,1)} %get-tuple-element.28) | copy-start | bytes 786436
  387.9 39.0 %slice-start.5 = ((s8[8388608]{0:T(1024)(128)(4,1)}), s8[4194304]{0:T(1024)(128)(4,1)S(1)}, s32[]{:S(2)}) async-start(s8[8388608]{0:T(1024)(128)(4,1)} %bitcast.89), calls=%async_computation.14 | async-start | bytes 8388608
  426.9 38.8 %slice-start.2 = ((s8[8388608]{0:T(1024)(128)(4,1)}), s8[4194304]{0:T(1024)(128)(4,1)S(1)}, s32[]{:S(2)}) async-start(s8[8388608]{0:T(1024)(128)(4,1)} %bitcast.87), calls=%async_computation.11 | async-start | bytes 8388608
  427.0 37.4 %copy-start.6 = (bf16[256,512]{1,0:T(8,128)(2,1)S(1)}, bf16[256,512]{1,0:T(8,128)(2,1)}, u32[]{:S(2)}) copy-start(bf16[256,512]{1,0:T(8,128)(2,1)} %get-tuple-element.27) | copy-start | bytes 786436
  427.0 38.8 %slice-start.3 = ((s8[8388608]{0:T(1024)(128)(4,1)}), s8[4194304]{0:T(1024)(128)(4,1)S(1)}, s32[]{:S(2)}) async-start(s8[8388608]{0:T(1024)(128)(4,1)} %bitcast.87), calls=%async_computation.12 | async-start | bytes 8388608
  465.7 38.7 %slice-start = ((s8[8388608]{0:T(1024)(128)(4,1)}), s8[4194304]{0:T(1024)(128)(4,1)S(1)}, s32[]{:S(2)}) async-start(s8[8388608]{0:T(1024)(128)(4,1)} %bitcast.85), calls=%async_computation.9 | async-start | bytes 8388608
  465.8 37.3 %copy-start.5 = (bf16[256,512]{1,0:T(8,128)(2,1)S(1)}, bf16[256,512]{1,0:T(8,128)(2,1)}, u32[]{:S(2)}) copy-start(bf16[256,512]{1,0:T(8,128)(2,1)} %get-tuple-element.26) | copy-start | bytes 786436
  465.8 38.7 %slice-start.1 = ((s8[8388608]{0:T(1024)(128)(4,1)}), s8[4194304]{0:T(1024)(128)(4,1)S(1)}, s32[]{:S(2)}) async-start(s8[8388608]{0:T(1024)(128)(4,1)} %bitcast.85), calls=%async_computation.10 | async-start | bytes 8388608
  504.5 36.6 %copy-start.4 = (f32[64,512]{1,0:T(8,128)S(1)}, f32[64,512]{1,0:T(8,128)}, u32[]{:S(2)}) copy-start(f32[64,512]{1,0:T(8,128)} %param.15) | copy-start | bytes 393220
  504.5 38.2 %copy-start.12 = (s32[64]{0:T(128)S(1)}, s32[64]{0:T(128)}, u32[]{:S(2)}) copy-start(s32[64]{0:T(128)} %param.22) | copy-start | bytes 772
Sparse Core Ops, SparseCore 0:
  13.6 67.3 reduce-scatter.12
  85.5 63.4 reduce-scatter.14
  152.7 63.1 reduce-scatter.16
  219.5 63.1 reduce-scatter.18
  307.0 77.4 all-reduce.2
where the time goes:
time: 593 us; the launch traced here: 588 us
  waiting for transfers between devices  265 us (45%)
  blocking collectives  164 us (28%)
  local copies, waits for them, and re-layouts  73.7 us (12%)
  matrix products  65.5 us (11%)
  between operations  14.4 us (2%)
    reduce_scatter x4, waiting for transfers between devices, split_factors(): lax.psum_scatter(jnp.dot(cholesky, correlate_source, precision=PRECISE),...  187 us
    all_gather x4, blocking collectives, split_factors(): lax.all_gather(shortened(ROOT_STEP * adjoint), 'factors', axis=0, tiled=T...  126 us
    psum x1, waiting for transfers between devices, split_factors(): lax.psum(partial_sum.astype(jnp.bfloat16), 'factors').astype(jnp.float32)  77.6 us
    gather x4, local copies, waits for them, and re-layouts, split_factors(): jnp.take(states[step_index + 1], local_factor, axis=0) - strike[:, None]  67.2 us
    psum x1, blocking collectives, per_device(): total_grad = lax.psum(slice_sums, ('paths', 'factors'))  37.8 us
    dot_general x4, matrix products, split_factors(): partial_sum = jnp.dot(set_table, values, preferred_element_type=jnp.float32)  25.3 us
    dot_general x4, matrix products, split_factors(): adjoint = adjoint + jnp.dot(factor_table, trade_term, precision=PRECISE)  21.5 us
  transfers between devices with their start and end apart: 5, of which 5 were waited for; matrix products, arithmetic and copies ran while one was open for 12% of the time, Pallas kernels for 0%

commit v1 on v0

--- a/solution.py
+++ b/solution.py
@@ -9,6 +9,11 @@
 DISCOUNT_RATE = 0.03
 PRECISE = lax.Precision.HIGHEST
 CONTRACT_FIRST = (((0,), (0,)), ((), ()))
+
+
+def gather_by_exchange(x, axis, dim):
+    copies = jnp.concatenate([x] * lax.axis_size(axis), axis=dim)
+    return lax.all_to_all(copies, axis, dim, dim, tiled=True)
 
 
 def shortened(value):
@@ -101,7 +106,7 @@
         adjoint = adjoint + jnp.dot(factor_table, trade_term, precision=PRECISE)
         shock_adjoint = jnp.zeros((factor_rows, path_cols), jnp.float32) + lax.dot_general(
             cholesky,
-            lax.all_gather(shortened(ROOT_STEP * adjoint), "factors", axis=0, tiled=True),
+            gather_by_exchange(shortened(ROOT_STEP * adjoint), "factors", 0),
             CONTRACT_FIRST,
             precision=PRECISE,
         )

time: 593 us -> 558 us (0.941)
  blocking collectives: 164 us -> 56.9 us
  waiting for transfers between devices: 265 us -> 294 us
  matrix products: 65.5 us -> 88.5 us
  local copies, waits for them, and re-layouts: 73.7 us -> 86.8 us
  starting transfers between devices: 0.5 us -> 11.7 us
    all_gather x4 -> x0, blocking collectives: 126 us -> none  [split_factors(): lax.all_gather(shortened(ROOT_STEP * adjoint), 'factors', axis=0, tiled=T...]
    all_to_all x0 -> x3, waiting for transfers between devices: none -> 29.2 us  [gather_by_exchange(): return lax.all_to_all(copies, axis, dim, dim, tiled=True)]
    all_to_all x0 -> x1, blocking collectives: none -> 18.1 us  [gather_by_exchange(): return lax.all_to_all(copies, axis, dim, dim, tiled=True)]
    dot_general x4, matrix products: 21.5 us -> 34.9 us  [split_factors(): adjoint = adjoint + jnp.dot(factor_table, trade_term, precision=PRECISE)]
    all_to_all x0 -> x3, starting transfers between devices: none -> 11.3 us  [gather_by_exchange(): return lax.all_to_all(copies, axis, dim, dim, tiled=True)]
    unnamed x42 -> x54, local copies, waits for them, and re-layouts: 6.53 us -> 17.7 us
    dot_general x4, matrix products: 6.62 us -> 16.3 us  [split_factors(): lax.dot_general(set_table, weights[step_index], CONTRACT_FIRST, preferred...]
  transfers between devices with their start and end apart: 5 -> 8, of which waited for: 5 -> 8; matrix products, arithmetic and copies ran while one was open for 12% -> 15% of each run, Pallas kernels for 0% -> 0%
where the time goes in v1:
time: 558 us; the launch traced here: 557 us
  waiting for transfers between devices  294 us (53%)
  matrix products  88.5 us (16%)
  local copies, waits for them, and re-layouts  86.8 us (16%)
  blocking collectives  56.9 us (10%)
  between operations  14.1 us (3%)
  starting transfers between devices  11.7 us (2%)
    reduce_scatter x4, waiting for transfers between devices, split_factors(): lax.psum_scatter(jnp.dot(cholesky, correlate_source, precision=PRECISE),...  187 us
    psum x1, waiting for transfers between devices, split_factors(): lax.psum(partial_sum.astype(jnp.bfloat16), 'factors').astype(jnp.float32)  77.5 us
    gather x4, local copies, waits for them, and re-layouts, split_factors(): jnp.take(states[step_index + 1], local_factor, axis=0) - strike[:, None]  67.2 us
    psum x1, blocking collectives, per_device(): total_grad = lax.psum(slice_sums, ('paths', 'factors'))  38.7 us
    dot_general x4, matrix products, split_factors(): adjoint = adjoint + jnp.dot(factor_table, trade_term, precision=PRECISE)  34.9 us
    all_to_all x3, waiting for transfers between devices, gather_by_exchange(): return lax.all_to_all(copies, axis, dim, dim, tiled=True)  29.2 us
    dot_general x4, matrix products, split_factors(): partial_sum = jnp.dot(set_table, values, preferred_element_type=jnp.float32)  25.3 us
    all_to_all x1, blocking collectives, gather_by_exchange(): return lax.all_to_all(copies, axis, dim, dim, tiled=True)  18.1 us
  transfers between devices with their start and end apart: 8, of which 8 were waited for; matrix products, arithmetic and copies ran while one was open for 15% of the time, Pallas kernels for 0%

profile of v1, /device:TPU:0, one launch (start us, length us, event | category | flops | bytes accessed | tf_op | source)
XLA Modules:
  0.0 557.0 jit_solution(15462284969064848836)
XLA Ops:
  7.2 0.9 convolution_bitcast_fusion.9
  8.2 0.9 convolution_bitcast_fusion.10
  9.1 0.9 broadcast_multiply_fusion.5
  10.0 2.1 convolution_bitcast_fusion.3
  12.1 1.3 copy.63
  13.5 0.7 multiply_subtract_fusion
  14.2 66.6 %reduce-scatter.13.cloned.1.call-done = f32[64,512]{1,0:T(8,128)} async-done(((f32[512,512]{1,0:T(8,128)}), f32[64,512]{1,0:T(8,128)}) %reduce-scatter.13.cloned.1.call-update) | async-done | bytes 131088 | tf_op jit(solution)/shard_map/reduce_scatter | solution.py:78
  80.8 1.0 multiply_add_fusion.4
  81.8 2.0 convolution_bitcast_fusion.2
  83.9 1.3 copy.65
  85.3 63.5 %reduce-scatter.15.cloned.1.call-done = f32[64,512]{1,0:T(8,128)} async-done(((f32[512,512]{1,0:T(8,128)}), f32[64,512]{1,0:T(8,128)}) %reduce-scatter.15.cloned.1.call-update) | async-done | bytes 131088 | tf_op jit(solution)/shard_map/reduce_scatter | solution.py:78
  148.8 1.0 multiply_add_fusion.3
  149.8 1.1 convolution_bitcast_fusion.1
  150.9 1.4 copy.67
  152.5 16.8 %gather_fusion.3 = f32[4096,512]{1,0:T(8,128)} fusion(f32[64,512]{1,0:T(8,128)S(1)} %multiply_add_fusion.4, s32[4096]{0:T(1024)S(1)} %fusion.166), kind=kCustom, calls=%fused_computation.3.clone | custom fusion | bytes 16793600 | tf_op jit(solution)/shard_map/jit(_take)/gather | solution.py:97
  169.3 46.4 %reduce-scatter.17.cloned.1.call-done = f32[64,512]{1,0:T(8,128)} async-done(((f32[512,512]{1,0:T(8,128)}), f32[64,512]{1,0:T(8,128)}) %reduce-scatter.17.cloned.1.call-update) | async-done | bytes 131088 | tf_op jit(solution)/shard_map/reduce_scatter | solution.py:78
  215.7 1.0 multiply_add_fusion.2
  216.7 1.1 convolution_bitcast_fusion
  217.8 1.4 copy.69
  219.5 6.3 %fusion.67 = bf16[256,512]{1,0:T(8,128)(2,1)} fusion(f32[4096,512]{1,0:T(8,128)} %gather_fusion.3, f32[4096]{0:T(1024)S(1)} %copy-done.10, f32[4096]{0:T(1024)S(1)} %copy-done.11, pred[4096]{0:T(1024)(128)(4,1)S(1)} %get-tuple-element.42, s32[4096]{0:T(1024)S(1)} %copy-done.3), kind=kOutput, calls=%fused_computation.80 | convolution fusion | flops 1083310080 | bytes 8704000 | tf_op jit(solution)/shard_map/dot_general | solution.py:89
  225.8 16.8 %gather_fusion.2 = f32[4096,512]{1,0:T(8,128)} fusion(f32[64,512]{1,0:T(8,128)S(1)} %multiply_add_fusion.3, s32[4096]{0:T(1024)S(1)} %fusion.166), kind=kCustom, calls=%fused_computation.2.clone | custom fusion | bytes 16793600 | tf_op jit(solution)/shard_map/jit(_take)/gather | solution.py:97
  242.6 6.3 %fusion.66 = bf16[256,512]{1,0:T(8,128)(2,1)} fusion(f32[4096,512]{1,0:T(8,128)} %gather_fusion.2, f32[4096]{0:T(1024)S(1)} %copy-done.10, f32[4096]{0:T(1024)S(1)} %copy-done.11, pred[4096]{0:T(1024)(128)(4,1)S(1)} %get-tuple-element.42, s32[4096]{0:T(1024)S(1)} %copy-done.3), kind=kOutput, calls=%fused_computation.79 | convolution fusion | flops 1083310080 | bytes 8704000 | tf_op jit(solution)/shard_map/dot_general | solution.py:89
  248.9 16.8 %gather_fusion.1 = f32[4096,512]{1,0:T(8,128)} fusion(f32[64,512]{1,0:T(8,128)S(1)} %multiply_add_fusion.2, s32[4096]{0:T(1024)S(1)} %fusion.166), kind=kCustom, calls=%fused_computation.1.clone | custom fusion | bytes 16793600 | tf_op jit(solution)/shard_map/jit(_take)/gather | solution.py:97
  265.7 6.4 %fusion.65 = bf16[256,512]{1,0:T(8,128)(2,1)} fusion(f32[4096,512]{1,0:T(8,128)} %gather_fusion.1, f32[4096]{0:T(1024)S(1)} %copy-done.10, f32[4096]{0:T(1024)S(1)} %copy-done.11, pred[4096]{0:T(1024)(128)(4,1)S(1)} %get-tuple-element.42, s32[4096]{0:T(1024)S(1)} %copy-done.3), kind=kOutput, calls=%fused_computation.78 | convolution fusion | flops 1083310080 | bytes 8704000 | tf_op jit(solution)/shard_map/dot_general | solution.py:89
  272.0 10.4 %reduce-scatter.19.cloned.1.call-done = f32[64,512]{1,0:T(8,128)} async-done(((f32[512,512]{1,0:T(8,128)}), f32[64,512]{1,0:T(8,128)}) %reduce-scatter.19.cloned.1.call-update) | async-done | bytes 131088 | tf_op jit(solution)/shard_map/reduce_scatter | solution.py:78
  282.4 1.0 multiply_add_fusion.1
  283.4 16.8 %gather_fusion = f32[4096,512]{1,0:T(8,128)} fusion(f32[64,512]{1,0:T(8,128)S(1)} %multiply_add_fusion.1, s32[4096]{0:T(1024)S(1)} %fusion.166), kind=kCustom, calls=%fused_computation.clone | custom fusion | bytes 16793600 | tf_op jit(solution)/shard_map/jit(_take)/gather | solution.py:97
  300.2 6.3 %fusion.64 = bf16[256,512]{1,0:T(8,128)(2,1)} fusion(f32[4096,512]{1,0:T(8,128)} %gather_fusion, f32[4096]{0:T(1024)S(1)} %copy-done.10, f32[4096]{0:T(1024)S(1)} %copy-done.11, pred[4096]{0:T(1024)(128)(4,1)S(1)} %get-tuple-element.42, s32[4096]{0:T(1024)S(1)} %copy-done.3), kind=kOutput, calls=%fused_computation.77 | convolution fusion | flops 1083310080 | bytes 8704000 | tf_op jit(solution)/shard_map/dot_general | solution.py:89
  306.6 77.5 %all-reduce.3.cloned.1.call-done = (bf16[256,512]{1,0:T(8,128)(2,1)}, bf16[256,512]{1,0:T(8,128)(2,1)}, bf16[256,512]{1,0:T(8,128)(2,1)}, bf16[256,512]{1,0:T(8,128)(2,1)}) async-done(((bf16[256,512]{1,0:T(8,128)(2,1)}, bf16[256,512]{1,0:T(8,128)(2,1)}, bf16[256,512]{1,0:T(8,128)(2,1)}, bf16[256,512]{1,0:T(8,128)(2,1)}), (bf16[256,512]{1,0:T(8,128)(2,1)}, bf16[256,512]{1,0:T(8,128)(2,1)}, ...) | async-done | bytes 1048592 | tf_op jit(solution)/shard_map/psum | solution.py:90
  384.0 2.5 fusion.38
  386.5 1.0 copy-done.1
  387.5 6.0 %constant_dynamic-update-slice_fusion.7 = (bf16[512,512]{1,0:T(8,128)(2,1)}, bf16[64,512]{1,0:T(8,128)(2,1)S(1)}, f32[64,512]{1,0:T(8,128)S(1)}) fusion(f32[4096,512]{1,0:T(8,128)S(1)} %fusion.38, f32[4096,512]{1,0:T(8,128)S(1)} %copy-done.1, f32[4096]{0:T(1024)S(1)} %copy-done.10, f32[4096]{0:T(1024)S(1)} %copy-done.11, ...), kind=kOutput, calls=%fused_computation.196 | convolution fusion | flops 1623523328 | bytes 17092608 | tf_op jit(solution)/shard_map/dot_general | solution.py:106
  393.5 0.6 constant_dynamic-update-slice_fusion.6
  394.1 0.6 constant_dynamic-update-slice_fusion.5
  394.7 0.6 constant_dynamic-update-slice_fusion.4
  395.4 0.6 constant_dynamic-update-slice_fusion.3
  396.6 0.6 constant_dynamic-update-slice_fusion.1
  397.2 0.6 constant_dynamic-update-slice_fusion
  397.8 4.0 all-to-all-start
  401.9 4.6 fusion.36
  406.5 9.5 %all-to-all-done = bf16[8,64,512]{2,1,0:T(8,128)(2,1)S(1)} async-done(((bf16[8,64,512]{2,1,0:T(8,128)(2,1)}), bf16[8,64,512]{2,1,0:T(8,128)(2,1)S(1)}, u32[]{:S(2)}, u32[]{:S(2)}) %all-to-all-start) | async-done | bytes 524320 | tf_op jit(solution)/shard_map/all_to_all | solution.py:16
  416.3 9.8 %constant_dynamic-update-slice_fusion.15 = (bf16[512,512]{1,0:T(8,128)(2,1)}, bf16[64,512]{1,0:T(8,128)(2,1)S(1)}, f32[64,512]{1,0:T(8,128)S(1)}) fusion(f32[4096,512]{1,0:T(8,128)} %fusion.36, f32[4096,512]{1,0:T(8,128)} %gather_fusion.1, f32[4096]{0:T(1024)S(1)} %copy-done.10, f32[4096]{0:T(1024)S(1)} %copy-done.11, ...), kind=kOutput, calls=%fused_computation.204 | convolution fusion | flops 1623851008 | bytes 17486848 | tf_op jit(solution)/shard_map/dot_general | solution.py:106
  426.2 0.6 constant_dynamic-update-slice_fusion.14
  427.4 0.6 constant_dynamic-update-slice_fusion.12
  428.0 0.6 constant_dynamic-update-slice_fusion.11
  429.3 0.6 constant_dynamic-update-slice_fusion.9
  429.9 0.6 constant_dynamic-update-slice_fusion.8
  430.5 3.6 all-to-all-start.1
  434.2 4.6 fusion.34
  438.8 9.7 %all-to-all-done.1 = bf16[8,64,512]{2,1,0:T(8,128)(2,1)S(1)} async-done(((bf16[8,64,512]{2,1,0:T(8,128)(2,1)}), bf16[8,64,512]{2,1,0:T(8,128)(2,1)S(1)}, u32[]{:S(2)}, u32[]{:S(2)}) %all-to-all-start.1) | async-done | bytes 524320 | tf_op jit(solution)/shard_map/all_to_all | solution.py:16
  448.9 9.8 %constant_dynamic-update-slice_fusion.23 = (bf16[512,512]{1,0:T(8,128)(2,1)}, bf16[64,512]{1,0:T(8,128)(2,1)S(1)}, f32[64,512]{1,0:T(8,128)S(1)}) fusion(f32[4096,512]{1,0:T(8,128)} %fusion.34, f32[4096,512]{1,0:T(8,128)} %gather_fusion.2, f32[4096]{0:T(1024)S(1)} %copy-done.10, f32[4096]{0:T(1024)S(1)} %copy-done.11, ...), kind=kOutput, calls=%fused_computation.212 | convolution fusion | flops 1623851008 | bytes 17486848 | tf_op jit(solution)/shard_map/dot_general | solution.py:106
  458.8 0.6 constant_dynamic-update-slice_fusion.22
  460.0 0.6 constant_dynamic-update-slice_fusion.20
  460.6 0.6 constant_dynamic-update-slice_fusion.19
  461.3 0.6 constant_dynamic-update-slice_fusion.18
  461.9 0.6 constant_dynamic-update-slice_fusion.17
  462.5 0.6 constant_dynamic-update-slice_fusion.16
  463.1 3.6 all-to-all-start.2
  466.8 4.6 fusion.32
  471.4 10.0 %all-to-all-done.2 = bf16[8,64,512]{2,1,0:T(8,128)(2,1)S(1)} async-done(((bf16[8,64,512]{2,1,0:T(8,128)(2,1)}), bf16[8,64,512]{2,1,0:T(8,128)(2,1)S(1)}, u32[]{:S(2)}, u32[]{:S(2)}) %all-to-all-start.2) | async-done | bytes 524320 | tf_op jit(solution)/shard_map/all_to_all | solution.py:16
  481.8 9.2 %constant_dynamic-update-slice_fusion.31 = (bf16[512,512]{1,0:T(8,128)(2,1)S(1)}, bf16[64,512]{1,0:T(8,128)(2,1)S(1)}, f32[64,512]{1,0:T(8,128)S(1)}) fusion(f32[4096,512]{1,0:T(8,128)} %fusion.32, f32[4096,512]{1,0:T(8,128)} %gather_fusion.3, f32[4096]{0:T(1024)S(1)} %copy-done.10, f32[4096]{0:T(1024)S(1)} %copy-done.11, ...), kind=kOutput, calls=%fused_computation.220 | convolution fusion | flops 1623851008 | bytes 17486848 | tf_op jit(solution)/shard_map/dot_general | solution.py:106
  491.2 18.1 %all_to_all.48 = bf16[8,64,512]{2,1,0:T(8,128)(2,1)S(1)} all-to-all(bf16[8,64,512]{2,1,0:T(8,128)(2,1)S(1)} %bitcast.97), channel_id=1, replica_groups=mesh['paths'=4,'factors'=8] {'factors'}, dimensions={0} | all-to-all | bytes 1048576 | tf_op jit(solution)/shard_map/all_to_all | solution.py:16
  509.3 1.6 fusion.100
  511.1 38.7 %psum.39 = f32[3,64]{1,0:T(4,128)S(1)} all-reduce(f32[3,64]{1,0:T(4,128)S(1)} %fusion.161), channel_id=1, replica_groups=mesh['paths'=4,'factors'=8] {'paths','factors'}, use_global_device_ids=true, to_apply=%region_20.22 | all-reduce | flops 192 | bytes 1536 | tf_op jit(solution)/shard_map/psum | solution.py:160
  (55 shorter events, 5.1 us)
Async XLA Ops:
  7.2 2.8 copy-start
  7.2 142.6 %copy-start.2 = (f32[4,64,512]{2,1,0:T(8,128)S(1)}, f32[4,64,512]{2,1,0:T(8,128)}, u32[]{:S(2)}) copy-start(f32[4,64,512]{2,1,0:T(8,128)} %param.16) | copy-start | bytes 1572868
  7.2 145.2 %copy-start.8 = (s32[4096]{0:T(1024)S(1)}, s32[4096]{0:T(1024)}, u32[]{:S(2)}) copy-start(s32[4096]{0:T(1024)} %param.26) | copy-start | bytes 49156
  7.2 73.6 %reduce-scatter.13.cloned.1.call-start = ((), (), s32[]{:S(2)}) async-start(), calls=%async_computation.8 | async-start | bytes 1179648 | tf_op jit(solution)/shard_map/reduce_scatter | solution.py:78
  13.5 135.4 %reduce-scatter.15.cloned.1.call-start = ((), (), s32[]{:S(2)}) async-start(), calls=%async_computation.9 | async-start | bytes 1179648 | tf_op jit(solution)/shard_map/reduce_scatter | solution.py:78
  85.2 130.4 %reduce-scatter.17.cloned.1.call-start = ((), (), s32[]{:S(2)}) async-start(), calls=%async_computation.10 | async-start | bytes 1179648 | tf_op jit(solution)/shard_map/reduce_scatter | solution.py:78
  152.4 130.0 %reduce-scatter.19.cloned.1.call-start = ((), (), s32[]{:S(2)}) async-start(), calls=%async_computation.11 | async-start | bytes 1179648 | tf_op jit(solution)/shard_map/reduce_scatter | solution.py:78
  152.5 67.0 %copy-start.3 = (s32[4096]{0:T(1024)S(1)}, s32[4096]{0:T(1024)}, u32[]{:S(2)}) copy-start(s32[4096]{0:T(1024)} %param.25) | copy-start | bytes 49156
  152.5 67.0 %copy-start.10 = (f32[4096]{0:T(1024)S(1)}, f32[4096]{0:T(1024)}, u32[]{:S(2)}) copy-start(f32[4096]{0:T(1024)} %param.24) | copy-start | bytes 49156
  152.5 67.0 %copy-start.11 = (f32[4096]{0:T(1024)S(1)}, f32[4096]{0:T(1024)}, u32[]{:S(2)}) copy-start(f32[4096]{0:T(1024)} %param.23) | copy-start | bytes 49156
  219.2 164.8 %all-reduce.3.cloned.1.call-start = ((), (), s32[]{:S(2)}) async-start(), calls=%async_computation.12 | async-start | bytes 2097152 | tf_op jit(solution)/shard_map/psum | solution.py:90
  300.2 6.4 %copy-start.9 = (f32[256]{0:T(256)S(1)}, f32[256]{0:T(256)}, u32[]{:S(2)}) copy-start(f32[256]{0:T(256)} %param.27) | copy-start | bytes 3076
  384.0 3.5 copy-start.1
  387.5 14.4 %copy-start.7 = (bf16[256,512]{1,0:T(8,128)(2,1)S(1)}, bf16[256,512]{1,0:T(8,128)(2,1)}, u32[]{:S(2)}) copy-start(bf16[256,512]{1,0:T(8,128)(2,1)} %get-tuple-element.30) | copy-start | bytes 786436
  397.8 18.1 %all-to-all-start = ((bf16[8,64,512]{2,1,0:T(8,128)(2,1)}), bf16[8,64,512]{2,1,0:T(8,128)(2,1)S(1)}, u32[]{:S(2)}, u32[]{:S(2)}) async-start(bf16[8,64,512]{2,1,0:T(8,128)(2,1)} %bitcast.14), calls=%async_computation | async-start | bytes 1048576 | tf_op jit(solution)/shard_map/all_to_all | solution.py:16
  416.3 17.8 %copy-start.6 = (bf16[256,512]{1,0:T(8,128)(2,1)S(1)}, bf16[256,512]{1,0:T(8,128)(2,1)}, u32[]{:S(2)}) copy-start(bf16[256,512]{1,0:T(8,128)(2,1)} %get-tuple-element.29) | copy-start | bytes 786436
  430.5 18.0 %all-to-all-start.1 = ((bf16[8,64,512]{2,1,0:T(8,128)(2,1)}), bf16[8,64,512]{2,1,0:T(8,128)(2,1)S(1)}, u32[]{:S(2)}, u32[]{:S(2)}) async-start(bf16[8,64,512]{2,1,0:T(8,128)(2,1)} %bitcast.17), calls=%async_computation.1 | async-start | bytes 1048576 | tf_op jit(solution)/shard_map/all_to_all | solution.py:16
  448.9 17.9 %copy-start.5 = (bf16[256,512]{1,0:T(8,128)(2,1)S(1)}, bf16[256,512]{1,0:T(8,128)(2,1)}, u32[]{:S(2)}) copy-start(bf16[256,512]{1,0:T(8,128)(2,1)} %get-tuple-element.28) | copy-start | bytes 786436
  463.1 18.3 %all-to-all-start.2 = ((bf16[8,64,512]{2,1,0:T(8,128)(2,1)}), bf16[8,64,512]{2,1,0:T(8,128)(2,1)S(1)}, u32[]{:S(2)}, u32[]{:S(2)}) async-start(bf16[8,64,512]{2,1,0:T(8,128)(2,1)} %bitcast.20), calls=%async_computation.2 | async-start | bytes 1048576 | tf_op jit(solution)/shard_map/all_to_all | solution.py:16
  481.8 27.5 %copy-start.4 = (f32[64,512]{1,0:T(8,128)S(1)}, f32[64,512]{1,0:T(8,128)}, u32[]{:S(2)}) copy-start(f32[64,512]{1,0:T(8,128)} %param.15) | copy-start | bytes 393220
  481.8 29.1 %copy-start.12 = (s32[64]{0:T(128)S(1)}, s32[64]{0:T(128)}, u32[]{:S(2)}) copy-start(s32[64]{0:T(128)} %param.22) | copy-start | bytes 772
Sparse Core Ops, SparseCore 0:
  13.6 67.1 reduce-scatter.12
  85.3 63.4 reduce-scatter.14
  152.5 63.1 reduce-scatter.16
  219.3 63.0 reduce-scatter.18
  306.7 77.3 all-reduce.2
